TPU v7x, 512 devices: a whole 4x8x8 slice. The times are simulated.
512 devices in a mesh: dp: 32 (over z_hi, y, core), seq: 16 (over z_lo, x).
Axes of the slice: x: 4, y: 8, z: 8 (z_hi: 2, z_lo: 4; z = z_hi * 4 + z_lo), core: 2. Of those that a mesh axis runs over, the one named last changes fastest.
Arguments:
- img_qkv: bfloat16 [32, 1792, 3, 2048], P('dp', 'seq'), may hold values from -6 to 6
- txt_qkv: bfloat16 [32, 256, 3, 2048], P('dp', 'seq'), may hold values from -6 to 6
- img_cot: bfloat16 [32, 1792, 2048], P('dp', 'seq'), may hold values from -48 to 48
- txt_cot: bfloat16 [32, 256, 2048], P('dp', 'seq'), may hold values from -48 to 48
- norm_gains: float32 [4, 128], replicated, may hold values from 0.5 to 2
Outputs:
- img_out: bfloat16 [32, 1792, 2048], P('dp', 'seq')
- txt_out: bfloat16 [32, 256, 2048], P('dp', 'seq')
- img_grad: bfloat16 [32, 1792, 3, 2048], P('dp', 'seq')
- txt_grad: bfloat16 [32, 256, 3, 2048], P('dp', 'seq')
- gain_grad: float32 [512], P('dp')
All inputs are finite; a program needn't handle non-finite values.
Results may differ from a plain program's by a relative error of at most 0.012.
The roundings to bfloat16 on the way count: a program that leaves them out, or rounds other values in their place, can miss the bound.
Values may be sent and summed in bfloat16 or wider, within the bound.
A program may use at most 128 MiB of HBM per device.

v0:
```python
import math
import jax
import jax.numpy as jnp
from jax import lax
from jax.sharding import PartitionSpec as P

HD = 128
GRID_W = 64
EPSILON = 1e-06


def rope_tables(seq_len, text_len, grid_w, head_dim):
    position = jnp.arange(seq_len, dtype=jnp.int32)
    image_pos = jnp.maximum(position - text_len, 0)
    image_col = (position >= text_len).astype(jnp.float32)
    row_pos = (image_pos // grid_w).astype(jnp.float32) * image_col
    col_pos = (image_pos % grid_w).astype(jnp.float32) * image_col
    time_dims = head_dim // 8
    axis_dims = (head_dim - time_dims) // 2
    channel = jnp.arange(head_dim, dtype=jnp.int32)
    in_rows = (channel >= time_dims) & (channel < time_dims + axis_dims)
    in_cols = channel >= time_dims + axis_dims
    within = jnp.where(in_cols, channel - time_dims - axis_dims, channel - time_dims)
    within = jnp.maximum(within, 0) // 2
    frequency = jnp.power(jnp.float32(10000.0), -2.0 * within.astype(jnp.float32) / axis_dims)
    angles = jnp.where(in_rows[None, :], row_pos[:, None] * frequency[None, :], jnp.float32(0.0))
    angles = jnp.where(in_cols[None, :], col_pos[:, None] * frequency[None, :], angles)
    even_lane = (channel % 2 == 0)[None, :]
    return (jnp.cos(angles), jnp.sin(angles), even_lane, image_col[:, None])


def rms_rows(values_in):
    inverse = lax.rsqrt(jnp.mean(values_in * values_in, axis=-1, keepdims=True) + EPSILON)
    return (values_in * inverse, inverse)


def rms_back(grad_hat, hat_vals, inverse):
    middle = jnp.mean(grad_hat * hat_vals, axis=-1, keepdims=True)
    return (grad_hat - hat_vals * middle) * inverse


def rotate(values_in, tables):
    cos_t, sin_t, even_lane, image_col = tables
    following = jnp.roll(values_in, -1, axis=-1)
    preceding = jnp.roll(values_in, 1, axis=-1)
    turned = jnp.where(even_lane, -following, preceding)
    return values_in * cos_t + turned * sin_t


def unrotate(grad_in, tables):
    cos_t, sin_t, even_lane, image_col = tables
    scaled = grad_in * sin_t
    following = jnp.roll(scaled, -1, axis=-1)
    preceding = jnp.roll(scaled, 1, axis=-1)
    turned = jnp.where(even_lane, following, -preceding)
    return grad_in * cos_t + turned


def head_pass(q_raw, k_raw, value, d_out, norm_gains, tables, n_blocks):
    image_col = tables[3]
    seq_len, head_dim = q_raw.shape
    attn_scale = 1.0 / math.sqrt(head_dim)
    q_hat, q_inv = rms_rows(q_raw)
    k_hat, k_inv = rms_rows(k_raw)
    q_gain = jnp.where(image_col > 0.5, norm_gains[0][None, :], norm_gains[2][None, :])
    k_gain = jnp.where(image_col > 0.5, norm_gains[1][None, :], norm_gains[3][None, :])
    q_rot = rotate(q_hat * q_gain, tables).astype(jnp.bfloat16)
    k_rot = rotate(k_hat * k_gain, tables).astype(jnp.bfloat16)
    block_rows = seq_len // n_blocks
    contract_last = (((1,), (1,)), ((), ()))
    contract_first = (((0,), (0,)), ((), ()))

    def block_step(pieces):
        q_block, d_block = pieces
        scores = (
            lax.dot_general(q_block, k_rot, contract_last, preferred_element_type=jnp.float32)
            * attn_scale
        )
        exp_scores = jnp.exp(scores)
        row_sum = jnp.sum(exp_scores, axis=1, keepdims=True)
        prob_half = (exp_scores / row_sum).astype(jnp.bfloat16)
        out_block = jnp.dot(prob_half, value, preferred_element_type=jnp.float32).astype(
            jnp.bfloat16
        )
        row_delta = jnp.sum(
            d_block.astype(jnp.float32) * out_block.astype(jnp.float32), axis=1, keepdims=True
        )
        d_prob = lax.dot_general(d_block, value, contract_last, preferred_element_type=jnp.float32)
        d_score = (exp_scores / row_sum * (d_prob - row_delta) * attn_scale).astype(jnp.bfloat16)
        return (out_block, prob_half, d_score)

    q_blocks = q_rot.reshape(n_blocks, block_rows, head_dim)
    d_blocks = d_out.reshape(n_blocks, block_rows, head_dim)
    out_blocks, prob_blocks, score_blocks = lax.map(block_step, (q_blocks, d_blocks))
    attn_out = out_blocks.reshape(seq_len, head_dim)
    prob_all = prob_blocks.reshape(seq_len, seq_len)
    d_score_all = score_blocks.reshape(seq_len, seq_len)
    d_value = lax.dot_general(prob_all, d_out, contract_first, preferred_element_type=jnp.float32)
    dq_rot = jnp.dot(d_score_all, k_rot, preferred_element_type=jnp.float32)
    dk_rot = lax.dot_general(d_score_all, q_rot, contract_first, preferred_element_type=jnp.float32)
    dq_norm = unrotate(dq_rot, tables)
    dk_norm = unrotate(dk_rot, tables)
    text_col = 1.0 - image_col
    gain_terms = jnp.stack(
        [
            jnp.sum(dq_norm * q_hat * image_col, axis=0),
            jnp.sum(dk_norm * k_hat * image_col, axis=0),
            jnp.sum(dq_norm * q_hat * text_col, axis=0),
            jnp.sum(dk_norm * k_hat * text_col, axis=0),
        ]
    )
    d_query = rms_back(dq_norm * q_gain, q_hat, q_inv).astype(jnp.bfloat16)
    d_key = rms_back(dk_norm * k_gain, k_hat, k_inv).astype(jnp.bfloat16)
    packed = jnp.stack([d_query, d_key, d_value.astype(jnp.bfloat16), attn_out], axis=1)
    return (packed, gain_terms)


def per_device(img_qkv, txt_qkv, img_cot, txt_cot, norm_gains):
    seq_devices = lax.axis_size("seq")
    data_devices = lax.axis_size("dp")
    img_proj, txt_proj = (
        lax.all_to_all(img_qkv, "seq", split_axis=3, concat_axis=1, tiled=True),
        lax.all_to_all(txt_qkv, "seq", split_axis=3, concat_axis=1, tiled=True),
    )
    img_grad_in, txt_grad_in = (
        lax.all_to_all(img_cot, "seq", split_axis=2, concat_axis=1, tiled=True),
        lax.all_to_all(txt_cot, "seq", split_axis=2, concat_axis=1, tiled=True),
    )
    text_len = txt_proj.shape[1]
    joint = jnp.concatenate([txt_proj[0], img_proj[0]], axis=0)
    joint_cot = jnp.concatenate([txt_grad_in[0], img_grad_in[0]], axis=0)
    seq_len = joint.shape[0]
    head_dim = HD
    local_heads = joint.shape[2] // head_dim
    tables = rope_tables(seq_len, text_len, GRID_W, head_dim)
    n_blocks = max(1, seq_len // 512)
    packed, gain_terms = head_pass(
        joint[:, 0, 0:head_dim].astype(jnp.float32),
        joint[:, 1, 0:head_dim].astype(jnp.float32),
        joint[:, 2, 0:head_dim],
        joint_cot,
        norm_gains,
        tables,
        n_blocks,
    )
    txt_back = packed[None, :text_len]
    img_back = packed[None, text_len:]
    img_tokens, txt_tokens = (
        lax.all_to_all(img_back, "seq", split_axis=1, concat_axis=3, tiled=True),
        lax.all_to_all(txt_back, "seq", split_axis=1, concat_axis=3, tiled=True),
    )
    img_out = img_tokens[:, :, 3, :]
    txt_out = txt_tokens[:, :, 3, :]
    img_grad = img_tokens[:, :, 0:3, :]
    txt_grad = txt_tokens[:, :, 0:3, :]
    grad_scale = 1.0 / math.sqrt(data_devices * seq_len * local_heads * seq_devices)
    partial_grad = (gain_terms * grad_scale).reshape(4 * head_dim)
    summed = lax.psum(partial_grad, "seq")
    gain_grad = lax.psum_scatter(summed, "dp", scatter_dimension=0, tiled=True)
    return (img_out, txt_out, img_grad, txt_grad, gain_grad)


def solution(mesh):
    in_specs = (
        P("dp", "seq", None, None),
        P("dp", "seq", None, None),
        P("dp", "seq", None),
        P("dp", "seq", None),
        P(),
    )
    out_specs = (
        P("dp", "seq", None),
        P("dp", "seq", None),
        P("dp", "seq", None, None),
        P("dp", "seq", None, None),
        P("dp"),
    )
    return jax.shard_map(
        per_device, mesh=mesh, in_specs=in_specs, out_specs=out_specs, check_vma=False
    )
```

profile of v0, /device:TPU:2, one launch (start us, length us, event | category | flops | bytes accessed | tf_op | source)
XLA Modules:
  0.0 398.8 jit_solution(10600250610665582752)
XLA Ops:
  3.1 11.5 %reduce.9 = bf16[2048,16]{1,0:T(8,128)(2,1)S(1)} reduce(bf16[2048,1,16]{2,1,0:T(2,128)(2,1)S(1)} %bitcast.205, bf16[]{:T(256)} %broadcast.812), dimensions={1}, to_apply=%bitcast.165.reduce_sub_computation | reduce | bytes 131074
  15.9 10.3 %all-to-all-start.2 = ((bf16[16,2,1024]{2,1,0:T(2,128)(2,1)}), bf16[16,2,1024]{2,1,0:T(2,128)(2,1)S(1)}, u32[]{:S(2)}, u32[]{:S(2)}) async-start(bf16[16,2,1024]{2,1,0:T(2,128)(2,1)} %reshape.852), calls=%async_computation.2 | async-start | bytes 131072 | tf_op jit(solution)/shard_map/all_to_all | solution.py:127
  33.2 6.0 %all-to-all-start = ((bf16[16,2,3072]{2,1,0:T(2,128)(2,1)}), bf16[16,2,3072]{2,1,0:T(2,128)(2,1)S(1)}, u32[]{:S(2)}, u32[]{:S(2)}) async-start(bf16[16,2,3072]{2,1,0:T(2,128)(2,1)} %reshape.848), calls=%async_computation | async-start | bytes 393216 | tf_op jit(solution)/shard_map/all_to_all | solution.py:123
  41.6 11.5 %reduce.8 = bf16[2048,112]{1,0:T(8,128)(2,1)S(1)} reduce(bf16[2048,1,112]{2,1,0:T(2,128)(2,1)S(1)} %bitcast.206, bf16[]{:T(256)} %broadcast.812), dimensions={1}, to_apply=%bitcast.163.reduce_sub_computation | reduce | bytes 917506
  55.0 7.7 %all-to-all-start.3 = ((bf16[16,2,7168]{2,1,0:T(2,128)(2,1)}), bf16[16,2,7168]{2,1,0:T(2,128)(2,1)S(1)}, u32[]{:S(2)}, u32[]{:S(2)}) async-start(bf16[16,2,7168]{2,1,0:T(2,128)(2,1)} %reshape.850), calls=%async_computation.3 | async-start | bytes 917504 | tf_op jit(solution)/shard_map/all_to_all | solution.py:126
  65.2 9.2 %all-to-all-done.3 = bf16[16,2,7168]{2,1,0:T(2,128)(2,1)S(1)} async-done(((bf16[16,2,7168]{2,1,0:T(2,128)(2,1)}), bf16[16,2,7168]{2,1,0:T(2,128)(2,1)S(1)}, u32[]{:S(2)}, u32[]{:S(2)}) %all-to-all-start.3) | async-done | bytes 458784 | tf_op jit(solution)/shard_map/all_to_all | solution.py:126
  75.1 6.0 %all-to-all-start.1 = ((bf16[1,112,3,2048]{1,2,0,3:T(4,128)(2,1)}), bf16[1,112,3,2048]{1,2,0,3:T(4,128)(2,1)S(1)}, u32[]{:S(2)}, u32[]{:S(2)}) async-start(bf16[1,112,3,2048]{1,2,0,3:T(4,128)(2,1)} %copy.60), calls=%async_computation.1 | async-start | bytes 4194304 | tf_op jit(solution)/shard_map/all_to_all | solution.py:122
  85.2 4.2 %reshape.849 = bf16[2048,1,3,16]{3,2,1,0:T(4,128)(2,1)} reshape(bf16[16,2,3072]{2,1,0:T(2,128)(2,1)} %copy-done.15) | data formatting | bytes 393216
  99.3 21.8 %all-to-all-done.1 = bf16[1,112,3,2048]{1,2,0,3:T(4,128)(2,1)S(1)} async-done(((bf16[1,112,3,2048]{1,2,0,3:T(4,128)(2,1)}), bf16[1,112,3,2048]{1,2,0,3:T(4,128)(2,1)S(1)}, u32[]{:S(2)}, u32[]{:S(2)}) %all-to-all-start.1) | async-done | bytes 1376288 | tf_op jit(solution)/shard_map/all_to_all | solution.py:122
  128.0 5.9 %fusion.33 = (bf16[2048,128]{0,1:T(8,128)(2,1)}, f32[2048,128]{0,1:T(8,128)S(1)}) fusion(f32[2048,1]{0,1:T(1,128)S(1)} %get-tuple-element.142, f32[2048,127]{0,1:T(8,128)S(1)} %get-tuple-element.145, f32[2048,127]{0,1:T(8,128)S(1)} %get-tuple-element.144, f32[2048,1]{0,1:T(1,128)S(1)} %get-tuple-element.141, f32[2048]{0:T(1024)S(1)} %get-tuple-element.161, ...), kind=kLoop, calls=%fused_computation.55 | loop fusion | flops 5242880 | bytes 4756352 | tf_op jit(solution)/shard_map/convert_element_type | solution.py:68
  150.0 7.8 %fusion.29 = bf16[4,512,128]{2,1,0:T(8,128)(2,1)S(1)} fusion(f32[4,512,1]{2,1,0:T(8,128)} %concatenate.120, f32[4,512,127]{2,1,0:T(8,128)} %bitcast.210, f32[4,512,127]{2,1,0:T(8,128)} %bitcast.211, f32[4,512,1]{2,1,0:T(8,128)} %concatenate.121, f32[4,512,128]{2,1,0:T(8,128)S(1)} %bitcast.209, f32[4,512]{1,0:T(4,128)S(1)} %copy-done.28, ...), kind=kLoop, calls=%fused_computation.50 | loop fusion | flops 3932160 | bytes 3698560 | tf_op jit(solution)/shard_map/convert_element_type | solution.py:67
  157.8 41.7 %while.14 = (s32[]{:T(128)}, bf16[4,512,128]{1,2,0:T(8,128)(2,1)}, bf16[4,512,2048]{2,1,0:T(8,128)(2,1)}, bf16[4,512,2048]{2,1,0:T(8,128)(2,1)}, bf16[4,512,128]...) while((s32[]{:T(128)}, bf16[4,512,128]{1,2,0:T(8,128)(2,1)}, ...), condition=%wide.region_5.6_spmd, body=%wide.region_2.5_spmd.sunk | while | flops 820313088 | bytes 65812748 | solution.py:94
  161.0 5.0 %fusion.134 = bf16[4,512,2048]{2,1,0:T(8,128)(2,1)} fusion(bf16[4,512,2048]{2,1,0:T(8,128)(2,1)} %get-tuple-element.237, s32[]{:T(128)} %get-tuple-element.234, bf16[2048,128]{1,0:T(8,128)(2,1)} %get-tuple-element.249, f32[512]{0:T(512)S(1)} %multiply_reduce_fusion.7, bf16[4,512,128]{2,1,0:T(8,128)(2,1)S(1)} %copy-done.2, ...), kind=kOutput, calls=%fused_computation.5.clone.1 | convolution fusion | flops 274726912 | bytes 6951936 | tf_op jit(solution)/shard_map/while/body/eval_jaxpr/dot_general | solution.py:88
  171.2 5.1 %fusion.134 = bf16[4,512,2048]{2,1,0:T(8,128)(2,1)} fusion(bf16[4,512,2048]{2,1,0:T(8,128)(2,1)} %get-tuple-element.237, s32[]{:T(128)} %get-tuple-element.234, bf16[2048,128]{1,0:T(8,128)(2,1)} %get-tuple-element.249, f32[512]{0:T(512)S(1)} %multiply_reduce_fusion.7, bf16[4,512,128]{2,1,0:T(8,128)(2,1)S(1)} %copy-done.2, ...), kind=kOutput, calls=%fused_computation.5.clone.1 | convolution fusion | flops 274726912 | bytes 6951936 | tf_op jit(solution)/shard_map/while/body/eval_jaxpr/dot_general | solution.py:88
  181.6 5.0 %fusion.134 = bf16[4,512,2048]{2,1,0:T(8,128)(2,1)} fusion(bf16[4,512,2048]{2,1,0:T(8,128)(2,1)} %get-tuple-element.237, s32[]{:T(128)} %get-tuple-element.234, bf16[2048,128]{1,0:T(8,128)(2,1)} %get-tuple-element.249, f32[512]{0:T(512)S(1)} %multiply_reduce_fusion.7, bf16[4,512,128]{2,1,0:T(8,128)(2,1)S(1)} %copy-done.2, ...), kind=kOutput, calls=%fused_computation.5.clone.1 | convolution fusion | flops 274726912 | bytes 6951936 | tf_op jit(solution)/shard_map/while/body/eval_jaxpr/dot_general | solution.py:88
  191.9 5.0 %fusion.134 = bf16[4,512,2048]{2,1,0:T(8,128)(2,1)} fusion(bf16[4,512,2048]{2,1,0:T(8,128)(2,1)} %get-tuple-element.237, s32[]{:T(128)} %get-tuple-element.234, bf16[2048,128]{1,0:T(8,128)(2,1)} %get-tuple-element.249, f32[512]{0:T(512)S(1)} %multiply_reduce_fusion.7, bf16[4,512,128]{2,1,0:T(8,128)(2,1)S(1)} %copy-done.2, ...), kind=kOutput, calls=%fused_computation.5.clone.1 | convolution fusion | flops 274726912 | bytes 6951936 | tf_op jit(solution)/shard_map/while/body/eval_jaxpr/dot_general | solution.py:88
  199.7 10.5 %fusion.57 = f32[2048,128]{0,1:T(8,128)S(1)} fusion(bf16[2048,2048]{1,0:T(8,128)(2,1)} %bitcast.232, bf16[2048,1,128]{0,2,1:T(8,128)(2,1)S(1)} %get-tuple-element.114, f32[2048,1,1]{0,2,1:T(1,128)} %get-tuple-element.140, f32[2048,1,127]{0,2,1:T(8,128)} %get-tuple-element.146, f32[2048,1,127]{0,2,1:T(8,128)S(1)} %copy-done.12, ...), kind=kOutput, calls=%fused_computation.97 | convolution fusion | flops 1077936128 | bytes 12087168 | tf_op jit(solution)/shard_map/dot_general | solution.py:99
  210.3 9.0 %fusion.47 = (f32[2048,128]{0,1:T(8,128)S(1)}, f32[2048,128]{0,1:T(8,128)S(1)}, f32[2048,128]{0,1:T(8,128)S(1)}) fusion(f32[2048]{0:T(1024)S(1)} %copy-done.26, f32[128]{0:T(128)S(1)} %copy-done.50, f32[2048]{0:T(1024)S(1)} %copy-done.24, pred[128]{0:T(512)(128)(4,1)S(1)} %copy-done.53, pred[128]{0:T(512)(128)(4,1)S(1)} %copy-done.47, ...), kind=kOutput, calls=%fused_computation.85 | convolution fusion | flops 1079508992 | bytes 15232896 | tf_op jit(solution)/shard_map/dot_general | solution.py:100
  220.0 9.2 %multiply_reduce_fusion.3 = (f32[128]{0:T(128)S(1)}, f32[128]{0:T(128)S(1)}, f32[2048]{0:T(1024)S(1)}, f32[2048]{0:T(1024)S(1)}, f32[128]{0:T(128)S(1)}, /*index...) fusion(bf16[2048,1,128]{0,2,1:T(8,128)(2,1)S(1)} %get-tuple-element.114, f32[2048]{0:T(1024)S(1)} %copy-done.29, ...), kind=kLoop, calls=%fused_computation.75 | loop fusion | flops 9956864 | bytes 9509760 | tf_op jit(solution)/shard_map/reduce_sum | solution.py:107
  235.5 12.1 %all-to-all-start.5 = ((bf16[1,256,4,128]{3,2,0,1:T(4,128)(2,1)}), bf16[1,256,4,128]{3,2,0,1:T(4,128)(2,1)S(1)}, u32[]{:S(2)}, u32[]{:S(2)}) async-start(bf16[1,256,4,128]{3,2,0,1:T(4,128)(2,1)} %copy.84), calls=%async_computation.5 | async-start | bytes 524288 | tf_op jit(solution)/shard_map/all_to_all | solution.py:150
  249.1 4.1 %copy.81 = bf16[1,1792,4,128]{3,2,0,1:T(4,128)(2,1)} copy(bf16[1,1792,4,128]{1,3,2,0:T(8,128)(2,1)} %slice_bitcast_fusion) | data formatting | bytes 3670016 | tf_op jit(solution)/shard_map/broadcast_in_dim | solution.py:147
  256.2 5.0 %all-to-all-start.4 = ((bf16[1,1792,4,128]{3,2,0,1:T(4,128)(2,1)}), bf16[1,1792,4,128]{3,2,0,1:T(4,128)(2,1)S(1)}, u32[]{:S(2)}, u32[]{:S(2)}) async-start(bf16[1,1792,4,128]{3,2,0,1:T(4,128)(2,1)} %copy.81), calls=%async_computation.4 | async-start | bytes 3670016 | tf_op jit(solution)/shard_map/all_to_all | solution.py:149
  263.1 92.2 %all-reduce = f32[512]{0:T(512)S(1)} all-reduce(f32[512]{0:T(512)S(1)} %fusion.101), channel_id=2, replica_groups=mesh['dp'=32,'seq'=16] {'dp'}, use_global_device_ids=true, to_apply=%region_13.14.clone | all-reduce | flops 512 | bytes 4096
  355.4 39.0 %psum.8 = f32[16]{0:T(128)} all-reduce(f32[16]{0:T(128)S(1)} %dynamic-slice.1), channel_id=1, replica_groups=mesh['dp'=32,'seq'=16] {'seq'}, use_global_device_ids=true, to_apply=%region_12.13 | all-reduce | flops 16 | bytes 128 | tf_op jit(solution)/shard_map/psum | solution.py:158
  (262 shorter events, 92.6 us)
Async XLA Ops:
  15.9 17.3 %all-to-all-start.2 = ((bf16[16,2,1024]{2,1,0:T(2,128)(2,1)}), bf16[16,2,1024]{2,1,0:T(2,128)(2,1)S(1)}, u32[]{:S(2)}, u32[]{:S(2)}) async-start(bf16[16,2,1024]{2,1,0:T(2,128)(2,1)} %reshape.852), calls=%async_computation.2 | async-start | bytes 131072 | tf_op jit(solution)/shard_map/all_to_all | solution.py:127
  28.7 33.9 %copy-start.11 = (bf16[1,112,3,2048]{3,1,2,0:T(8,128)(2,1)S(1)}, bf16[1,112,3,2048]{3,1,2,0:T(8,128)(2,1)}, u32[]{:S(2)}) copy-start(bf16[1,112,3,2048]{3,1,2,0:T(8,128)(2,1)} %param.7) | copy-start | bytes 4128772
  33.2 21.8 %all-to-all-start = ((bf16[16,2,3072]{2,1,0:T(2,128)(2,1)}), bf16[16,2,3072]{2,1,0:T(2,128)(2,1)S(1)}, u32[]{:S(2)}, u32[]{:S(2)}) async-start(bf16[16,2,3072]{2,1,0:T(2,128)(2,1)} %reshape.848), calls=%async_computation | async-start | bytes 393216 | tf_op jit(solution)/shard_map/all_to_all | solution.py:123
  55.0 28.7 %copy-start.57 = (f32[4,128]{1,0:T(4,128)S(1)}, f32[4,128]{1,0:T(4,128)}, u32[]{:S(2)}) copy-start(f32[4,128]{1,0:T(4,128)} %param.11) | copy-start | bytes 6148
  55.0 19.4 %copy-start.15 = (bf16[16,2,3072]{2,1,0:T(2,128)(2,1)}, bf16[16,2,3072]{2,1,0:T(2,128)(2,1)S(1)}, u32[]{:S(2)}) copy-start(bf16[16,2,3072]{2,1,0:T(2,128)(2,1)S(1)} %all-to-all-done) | copy-start | bytes 589828
  55.0 19.4 %all-to-all-start.3 = ((bf16[16,2,7168]{2,1,0:T(2,128)(2,1)}), bf16[16,2,7168]{2,1,0:T(2,128)(2,1)S(1)}, u32[]{:S(2)}, u32[]{:S(2)}) async-start(bf16[16,2,7168]{2,1,0:T(2,128)(2,1)} %reshape.850), calls=%async_computation.3 | async-start | bytes 917504 | tf_op jit(solution)/shard_map/all_to_all | solution.py:126
  75.1 45.9 %all-to-all-start.1 = ((bf16[1,112,3,2048]{1,2,0,3:T(4,128)(2,1)}), bf16[1,112,3,2048]{1,2,0,3:T(4,128)(2,1)S(1)}, u32[]{:S(2)}, u32[]{:S(2)}) async-start(bf16[1,112,3,2048]{1,2,0,3:T(4,128)(2,1)} %copy.60), calls=%async_computation.1 | async-start | bytes 4194304 | tf_op jit(solution)/shard_map/all_to_all | solution.py:122
  81.2 46.7 %copy-start.45 = (pred[128]{0:T(512)(128)(4,1)}, pred[128]{0:T(512)(128)(4,1)S(1)}, u32[]{:S(2)}) copy-start(pred[128]{0:T(512)(128)(4,1)S(1)} %iota_compare_fusion.1) | copy-start | bytes 388
  81.2 46.7 %copy-start.48 = (f32[128]{0:T(128)}, f32[128]{0:T(128)S(1)}, u32[]{:S(2)}) copy-start(f32[128]{0:T(128)S(1)} %multiply_power_fusion) | copy-start | bytes 1540
  81.2 46.6 %copy-start.51 = (pred[128]{0:T(512)(128)(4,1)}, pred[128]{0:T(512)(128)(4,1)S(1)}, u32[]{:S(2)}) copy-start(pred[128]{0:T(512)(128)(4,1)S(1)} %get-tuple-element.162) | copy-start | bytes 388
  81.3 46.6 %copy-start.54 = (pred[128]{0:T(512)(128)(4,1)}, pred[128]{0:T(512)(128)(4,1)S(1)}, u32[]{:S(2)}) copy-start(pred[128]{0:T(512)(128)(4,1)S(1)} %get-tuple-element.163) | copy-start | bytes 388
  83.0 44.9 %copy-start.23 = (f32[2048]{0:T(1024)}, f32[2048]{0:T(1024)S(1)}, u32[]{:S(2)}) copy-start(f32[2048]{0:T(1024)S(1)} %get-tuple-element.160) | copy-start | bytes 24580
  83.0 44.9 %copy-start.25 = (f32[2048]{0:T(1024)}, f32[2048]{0:T(1024)S(1)}, u32[]{:S(2)}) copy-start(f32[2048]{0:T(1024)S(1)} %get-tuple-element.161) | copy-start | bytes 24580
  83.7 44.2 %copy-start.31 = (f32[128]{0:T(128)}, f32[128]{0:T(128)S(1)}, u32[]{:S(2)}) copy-start(f32[128]{0:T(128)S(1)} %get-tuple-element.153) | copy-start | bytes 1540
  83.7 44.2 %copy-start.33 = (f32[128]{0:T(128)}, f32[128]{0:T(128)S(1)}, u32[]{:S(2)}) copy-start(f32[128]{0:T(128)S(1)} %get-tuple-element.154) | copy-start | bytes 1540
  83.7 44.2 %copy-start.36 = (f32[128]{0:T(128)}, f32[128]{0:T(128)S(1)}, u32[]{:S(2)}) copy-start(f32[128]{0:T(128)S(1)} %get-tuple-element.155) | copy-start | bytes 1540
  83.7 44.2 %copy-start.40 = (f32[128]{0:T(128)}, f32[128]{0:T(128)S(1)}, u32[]{:S(2)}) copy-start(f32[128]{0:T(128)S(1)} %get-tuple-element.156) | copy-start | bytes 1540
  85.2 12.4 %copy-start.18 = (bf16[1,16,16,128]{3,2,1,0:T(8,128)(2,1)}, bf16[1,16,16,128]{3,2,1,0:T(8,128)(2,1)S(1)}, u32[]{:S(2)}) copy-start(bf16[1,16,16,128]{3,2,1,0:T(8,128)(2,1)S(1)} %copy.72) | copy-start | bytes 196612
  92.3 32.8 %copy-start.10 = (bf16[256,3,128]{0,2,1:T(8,128)(2,1)}, bf16[256,3,128]{0,2,1:T(8,128)(2,1)S(1)}, u32[]{:S(2)}) copy-start(bf16[256,3,128]{0,2,1:T(8,128)(2,1)S(1)} %copy.63) | copy-start | bytes 589828
  138.7 11.3 %copy-start.37 = (f32[128]{0:T(128)S(1)}, f32[128]{0:T(128)}, u32[]{:S(2)}) copy-start(f32[128]{0:T(128)} %copy-done.36) | copy-start | bytes 1540
  138.7 11.3 %copy-start.42 = (pred[4,512]{1,0:T(4,128)(4,1)S(1)}, pred[4,512]{1,0:T(4,128)(4,1)}, u32[]{:S(2)}) copy-start(pred[4,512]{1,0:T(4,128)(4,1)} %convert_compare_fusion) | copy-start | bytes 6148
  157.8 41.7 %copy-start.12 = (f32[2048,1,127]{0,2,1:T(8,128)S(1)}, f32[2048,1,127]{0,2,1:T(8,128)}, u32[]{:S(2)}) copy-start(f32[2048,1,127]{0,2,1:T(8,128)} %get-tuple-element.143) | copy-start | bytes 3121156
  235.5 20.7 %all-to-all-start.5 = ((bf16[1,256,4,128]{3,2,0,1:T(4,128)(2,1)}), bf16[1,256,4,128]{3,2,0,1:T(4,128)(2,1)S(1)}, u32[]{:S(2)}, u32[]{:S(2)}) async-start(bf16[1,256,4,128]{3,2,0,1:T(4,128)(2,1)} %copy.84), calls=%async_computation.5 | async-start | bytes 524288 | tf_op jit(solution)/shard_map/all_to_all | solution.py:150
  256.2 139.6 %all-to-all-start.4 = ((bf16[1,1792,4,128]{3,2,0,1:T(4,128)(2,1)}), bf16[1,1792,4,128]{3,2,0,1:T(4,128)(2,1)S(1)}, u32[]{:S(2)}, u32[]{:S(2)}) async-start(bf16[1,1792,4,128]{3,2,0,1:T(4,128)(2,1)} %copy.81), calls=%async_computation.4 | async-start | bytes 3670016 | tf_op jit(solution)/shard_map/all_to_all | solution.py:149
  (61 other events, 352.0 us)
where the time goes:
time: 406 us; the launch traced here: 399 us
  blocking collectives  131 us (32%)
  local copies, waits for them, and re-layouts  67.2 us (17%)
  other arithmetic  62.7 us (15%)
  matrix products  51.8 us (13%)
  starting transfers between devices  47.1 us (12%)
  waiting for transfers between devices  35.8 us (9%)
    unnamed x1, blocking collectives  92.2 us
    psum x1, blocking collectives, per_device(): summed = lax.psum(partial_grad, 'seq')  39 us
    unnamed x125, local copies, waits for them, and re-layouts  27.8 us
    unnamed x3, other arithmetic  23.1 us
    all_to_all x1, waiting for transfers between devices, per_device(): lax.all_to_all(img_qkv, 'seq', split_axis=3, concat_axis=1, tiled=True)  21.8 us
    dot_general x4, matrix products, block_step(): lax.dot_general(d_block, value, contract_last, preferred_element_type=jnp...  20.2 us
    all_to_all x1, starting transfers between devices, per_device(): lax.all_to_all(txt_back, 'seq', split_axis=1, concat_axis=3, tiled=True)  12.1 us
    dot_general x1, matrix products, head_pass(): dq_rot = jnp.dot(d_score_all, k_rot, preferred_element_type=jnp.float32)  10.5 us
  transfers between devices with their start and end apart: 6, of which 4 were waited for; matrix products, arithmetic and copies ran while one was open for 12% of the time, Pallas kernels for 0%

commit v1 on v0

--- a/solution.py
+++ b/solution.py
@@ -155,7 +155,7 @@
     txt_grad = txt_tokens[:, :, 0:3, :]
     grad_scale = 1.0 / math.sqrt(data_devices * seq_len * local_heads * seq_devices)
     partial_grad = (gain_terms * grad_scale).reshape(4 * head_dim)
-    summed = lax.psum(partial_grad, "seq")
+    summed = jnp.sum(lax.all_gather(partial_grad, "seq"), axis=0)
     gain_grad = lax.psum_scatter(summed, "dp", scatter_dimension=0, tiled=True)
     return (img_out, txt_out, img_grad, txt_grad, gain_grad)
 

time: 406 us -> 424 us (1.044)
  the two profiles are of different devices: /device:TPU:2 before, /device:TPU:128 now
where the time goes in v1:
time: 424 us; the launch traced here: 417 us
  blocking collectives  150 us (35%)
  local copies, waits for them, and re-layouts  66.6 us (16%)
  other arithmetic  62.9 us (15%)
  matrix products  51.9 us (12%)
  waiting for transfers between devices  42.6 us (10%)
  starting transfers between devices  39.9 us (9%)
    unnamed x1, blocking collectives  86 us
    all_gather x1, blocking collectives, per_device(): summed = jnp.sum(lax.all_gather(partial_grad, 'seq'), axis=0)  64.4 us
    all_to_all x1, waiting for transfers between devices, per_device(): lax.all_to_all(img_qkv, 'seq', split_axis=3, concat_axis=1, tiled=True)  31.6 us
    unnamed x107, local copies, waits for them, and re-layouts  27.2 us
    unnamed x3, other arithmetic  23.1 us
    dot_general x4, matrix products, block_step(): lax.dot_general(d_block, value, contract_last, preferred_element_type=jnp...  20.2 us
    dot_general x1, matrix products, head_pass(): dq_rot = jnp.dot(d_score_all, k_rot, preferred_element_type=jnp.float32)  10.5 us
    concatenate x6, local copies, waits for them, and re-layouts, rotate(): preceding = jnp.roll(values_in, 1, axis=-1)  9.45 us
  transfers between devices with their start and end apart: 6, of which 4 were waited for; matrix products, arithmetic and copies ran while one was open for 12% of the time, Pallas kernels for 0%

profile of v1, /device:TPU:128, one launch (start us, length us, event | category | flops | bytes accessed | tf_op | source)
XLA Modules:
  0.0 417.4 jit_solution(6558847438648021533)
XLA Ops:
  3.1 11.5 %reduce.10 = bf16[2048,16]{1,0:T(8,128)(2,1)S(1)} reduce(bf16[2048,1,16]{2,1,0:T(2,128)(2,1)S(1)} %bitcast.204, bf16[]{:T(256)} %broadcast.818), dimensions={1}, to_apply=%bitcast.164.reduce_sub_computation | reduce | bytes 131074
  15.9 8.5 %all-to-all-start.2 = ((bf16[16,2,1024]{2,1,0:T(2,128)(2,1)}), bf16[16,2,1024]{2,1,0:T(2,128)(2,1)S(1)}, u32[]{:S(2)}, u32[]{:S(2)}) async-start(bf16[16,2,1024]{2,1,0:T(2,128)(2,1)} %reshape.863), calls=%async_computation.2 | async-start | bytes 131072 | tf_op jit(solution)/shard_map/all_to_all | solution.py:127
  30.1 7.3 %all-to-all-start = ((bf16[16,2,3072]{2,1,0:T(2,128)(2,1)}), bf16[16,2,3072]{2,1,0:T(2,128)(2,1)S(1)}, u32[]{:S(2)}, u32[]{:S(2)}) async-start(bf16[16,2,3072]{2,1,0:T(2,128)(2,1)} %reshape.859), calls=%async_computation | async-start | bytes 393216 | tf_op jit(solution)/shard_map/all_to_all | solution.py:123
  39.8 11.5 %reduce.9 = bf16[2048,112]{1,0:T(8,128)(2,1)S(1)} reduce(bf16[2048,1,112]{2,1,0:T(2,128)(2,1)S(1)} %bitcast.205, bf16[]{:T(256)} %broadcast.818), dimensions={1}, to_apply=%bitcast.162.reduce_sub_computation | reduce | bytes 917506
  53.2 7.7 %all-to-all-start.3 = ((bf16[16,2,7168]{2,1,0:T(2,128)(2,1)}), bf16[16,2,7168]{2,1,0:T(2,128)(2,1)S(1)}, u32[]{:S(2)}, u32[]{:S(2)}) async-start(bf16[16,2,7168]{2,1,0:T(2,128)(2,1)} %reshape.861), calls=%async_computation.3 | async-start | bytes 917504 | tf_op jit(solution)/shard_map/all_to_all | solution.py:126
  60.8 4.1 copy.60
  64.9 7.9 %all-to-all-done.3 = bf16[16,2,7168]{2,1,0:T(2,128)(2,1)S(1)} async-done(((bf16[16,2,7168]{2,1,0:T(2,128)(2,1)}), bf16[16,2,7168]{2,1,0:T(2,128)(2,1)S(1)}, u32[]{:S(2)}, u32[]{:S(2)}) %all-to-all-start.3) | async-done | bytes 458784 | tf_op jit(solution)/shard_map/all_to_all | solution.py:126
  72.9 5.7 %all-to-all-start.1 = ((bf16[1,112,3,2048]{1,2,0,3:T(4,128)(2,1)}), bf16[1,112,3,2048]{1,2,0,3:T(4,128)(2,1)S(1)}, u32[]{:S(2)}, u32[]{:S(2)}) async-start(bf16[1,112,3,2048]{1,2,0,3:T(4,128)(2,1)} %copy.60), calls=%async_computation.1 | async-start | bytes 4194304 | tf_op jit(solution)/shard_map/all_to_all | solution.py:122
  93.8 31.6 %all-to-all-done.1 = bf16[1,112,3,2048]{1,2,0,3:T(4,128)(2,1)S(1)} async-done(((bf16[1,112,3,2048]{1,2,0,3:T(4,128)(2,1)}), bf16[1,112,3,2048]{1,2,0,3:T(4,128)(2,1)S(1)}, u32[]{:S(2)}, u32[]{:S(2)}) %all-to-all-start.1) | async-done | bytes 1376288 | tf_op jit(solution)/shard_map/all_to_all | solution.py:122
  132.3 6.0 %fusion.33 = (bf16[2048,128]{0,1:T(8,128)(2,1)}, f32[2048,128]{0,1:T(8,128)S(1)}) fusion(f32[2048,1]{0,1:T(1,128)S(1)} %get-tuple-element.142, f32[2048,127]{0,1:T(8,128)S(1)} %get-tuple-element.145, f32[2048,127]{0,1:T(8,128)S(1)} %get-tuple-element.144, f32[2048,1]{0,1:T(1,128)S(1)} %get-tuple-element.141, f32[2048]{0:T(1024)S(1)} %get-tuple-element.161, ...), kind=kLoop, calls=%fused_computation.55 | loop fusion | flops 5242880 | bytes 4756352 | tf_op jit(solution)/shard_map/convert_element_type | solution.py:68
  154.3 7.8 %fusion.29 = bf16[4,512,128]{2,1,0:T(8,128)(2,1)S(1)} fusion(f32[4,512,1]{2,1,0:T(8,128)} %concatenate.120, f32[4,512,127]{2,1,0:T(8,128)} %bitcast.209, f32[4,512,127]{2,1,0:T(8,128)} %bitcast.210, f32[4,512,1]{2,1,0:T(8,128)} %concatenate.121, f32[4,512,128]{2,1,0:T(8,128)S(1)} %bitcast.208, f32[4,512]{1,0:T(4,128)S(1)} %get-tuple-element.165, ...), kind=kLoop, calls=%fused_computation.50 | loop fusion | flops 3932160 | bytes 3698560 | tf_op jit(solution)/shard_map/convert_element_type | solution.py:67
  162.1 41.9 %while.14 = (s32[]{:T(128)}, bf16[4,512,128]{1,2,0:T(8,128)(2,1)}, bf16[4,512,2048]{2,1,0:T(8,128)(2,1)}, bf16[4,512,2048]{2,1,0:T(8,128)(2,1)}, bf16[4,512,128]...) while((s32[]{:T(128)}, bf16[4,512,128]{1,2,0:T(8,128)(2,1)}, ...), condition=%wide.region_5.6_spmd, body=%wide.region_2.5_spmd.sunk | while | flops 820313088 | bytes 65812748 | solution.py:94
  165.3 5.1 %fusion.133 = bf16[4,512,2048]{2,1,0:T(8,128)(2,1)} fusion(bf16[4,512,2048]{2,1,0:T(8,128)(2,1)} %get-tuple-element.237, s32[]{:T(128)} %get-tuple-element.234, bf16[2048,128]{1,0:T(8,128)(2,1)} %get-tuple-element.249, f32[512]{0:T(512)S(1)} %multiply_reduce_fusion.7, bf16[4,512,128]{2,1,0:T(8,128)(2,1)S(1)} %copy-done.3, ...), kind=kOutput, calls=%fused_computation.5.clone.1 | convolution fusion | flops 274726912 | bytes 6951936 | tf_op jit(solution)/shard_map/while/body/eval_jaxpr/dot_general | solution.py:88
  175.6 5.1 %fusion.133 = bf16[4,512,2048]{2,1,0:T(8,128)(2,1)} fusion(bf16[4,512,2048]{2,1,0:T(8,128)(2,1)} %get-tuple-element.237, s32[]{:T(128)} %get-tuple-element.234, bf16[2048,128]{1,0:T(8,128)(2,1)} %get-tuple-element.249, f32[512]{0:T(512)S(1)} %multiply_reduce_fusion.7, bf16[4,512,128]{2,1,0:T(8,128)(2,1)S(1)} %copy-done.3, ...), kind=kOutput, calls=%fused_computation.5.clone.1 | convolution fusion | flops 274726912 | bytes 6951936 | tf_op jit(solution)/shard_map/while/body/eval_jaxpr/dot_general | solution.py:88
  186.0 5.0 %fusion.133 = bf16[4,512,2048]{2,1,0:T(8,128)(2,1)} fusion(bf16[4,512,2048]{2,1,0:T(8,128)(2,1)} %get-tuple-element.237, s32[]{:T(128)} %get-tuple-element.234, bf16[2048,128]{1,0:T(8,128)(2,1)} %get-tuple-element.249, f32[512]{0:T(512)S(1)} %multiply_reduce_fusion.7, bf16[4,512,128]{2,1,0:T(8,128)(2,1)S(1)} %copy-done.3, ...), kind=kOutput, calls=%fused_computation.5.clone.1 | convolution fusion | flops 274726912 | bytes 6951936 | tf_op jit(solution)/shard_map/while/body/eval_jaxpr/dot_general | solution.py:88
  196.3 5.0 %fusion.133 = bf16[4,512,2048]{2,1,0:T(8,128)(2,1)} fusion(bf16[4,512,2048]{2,1,0:T(8,128)(2,1)} %get-tuple-element.237, s32[]{:T(128)} %get-tuple-element.234, bf16[2048,128]{1,0:T(8,128)(2,1)} %get-tuple-element.249, f32[512]{0:T(512)S(1)} %multiply_reduce_fusion.7, bf16[4,512,128]{2,1,0:T(8,128)(2,1)S(1)} %copy-done.3, ...), kind=kOutput, calls=%fused_computation.5.clone.1 | convolution fusion | flops 274726912 | bytes 6951936 | tf_op jit(solution)/shard_map/while/body/eval_jaxpr/dot_general | solution.py:88
  204.1 10.5 %fusion.57 = f32[2048,128]{0,1:T(8,128)S(1)} fusion(bf16[2048,2048]{1,0:T(8,128)(2,1)} %bitcast.232, bf16[2048,1,128]{0,2,1:T(8,128)(2,1)S(1)} %get-tuple-element.114, f32[2048,1,1]{0,2,1:T(1,128)} %get-tuple-element.140, f32[2048,1,127]{0,2,1:T(8,128)} %get-tuple-element.146, f32[2048,1,127]{0,2,1:T(8,128)S(1)} %copy-done.12, ...), kind=kOutput, calls=%fused_computation.97 | convolution fusion | flops 1077936128 | bytes 12087168 | tf_op jit(solution)/shard_map/dot_general | solution.py:99
  214.7 9.1 %fusion.47 = (f32[2048,128]{0,1:T(8,128)S(1)}, f32[2048,128]{0,1:T(8,128)S(1)}, f32[2048,128]{0,1:T(8,128)S(1)}) fusion(f32[2048]{0:T(1024)S(1)} %copy-done.25, f32[128]{0:T(128)S(1)} %copy-done.42, f32[2048]{0:T(1024)S(1)} %copy-done.23, pred[128]{0:T(512)(128)(4,1)S(1)} %copy-done.44, pred[128]{0:T(512)(128)(4,1)S(1)} %copy-done.40, ...), kind=kOutput, calls=%fused_computation.85 | convolution fusion | flops 1079508992 | bytes 15232896 | tf_op jit(solution)/shard_map/dot_general | solution.py:100
  224.6 9.2 %multiply_reduce_fusion.3 = (f32[128]{0:T(128)S(1)}, f32[128]{0:T(128)S(1)}, f32[2048]{0:T(1024)S(1)}, f32[2048]{0:T(1024)S(1)}, f32[128]{0:T(128)S(1)}, /*index...) fusion(bf16[2048,1,128]{0,2,1:T(8,128)(2,1)S(1)} %get-tuple-element.114, f32[2048]{0:T(1024)S(1)} %copy-done.26, ...), kind=kLoop, calls=%fused_computation.75 | loop fusion | flops 9956864 | bytes 9509760 | tf_op jit(solution)/shard_map/reduce_sum | solution.py:107
  241.3 5.2 %all-to-all-start.5 = ((bf16[1,256,4,128]{3,2,0,1:T(4,128)(2,1)}), bf16[1,256,4,128]{3,2,0,1:T(4,128)(2,1)S(1)}, u32[]{:S(2)}, u32[]{:S(2)}) async-start(bf16[1,256,4,128]{3,2,0,1:T(4,128)(2,1)} %copy.84), calls=%async_computation.5 | async-start | bytes 524288 | tf_op jit(solution)/shard_map/all_to_all | solution.py:150
  247.8 4.1 copy.81
  254.5 5.6 %all-to-all-start.4 = ((bf16[1,1792,4,128]{3,2,0,1:T(4,128)(2,1)}), bf16[1,1792,4,128]{3,2,0,1:T(4,128)(2,1)S(1)}, u32[]{:S(2)}, u32[]{:S(2)}) async-start(bf16[1,1792,4,128]{3,2,0,1:T(4,128)(2,1)} %copy.81), calls=%async_computation.4 | async-start | bytes 3670016 | tf_op jit(solution)/shard_map/all_to_all | solution.py:149
  262.0 64.4 %all-gather = f32[16,1,512]{2,1,0:T(1,128)S(1)} all-gather(f32[1,1,512]{2,1,0:T(1,128)S(1)} %bitcast.224), channel_id=1, replica_groups=mesh['dp'=32,'seq'=16] {'seq'}, dimensions={0}, use_global_device_ids=true | all-gather | bytes 34816 | tf_op jit(solution)/shard_map/all_gather | solution.py:158
  326.5 86.0 %all-reduce = f32[512]{0:T(512)S(1)} all-reduce(f32[512]{0:T(512)S(1)} %reduce_sum.107), channel_id=2, replica_groups=mesh['dp'=32,'seq'=16] {'dp'}, use_global_device_ids=true, to_apply=%region_13.14.clone | all-reduce | flops 512 | bytes 4096
  (245 shorter events, 90.5 us)
Async XLA Ops:
  15.9 14.3 %all-to-all-start.2 = ((bf16[16,2,1024]{2,1,0:T(2,128)(2,1)}), bf16[16,2,1024]{2,1,0:T(2,128)(2,1)S(1)}, u32[]{:S(2)}, u32[]{:S(2)}) async-start(bf16[16,2,1024]{2,1,0:T(2,128)(2,1)} %reshape.863), calls=%async_computation.2 | async-start | bytes 131072 | tf_op jit(solution)/shard_map/all_to_all | solution.py:127
  30.1 23.0 %all-to-all-start = ((bf16[16,2,3072]{2,1,0:T(2,128)(2,1)}), bf16[16,2,3072]{2,1,0:T(2,128)(2,1)S(1)}, u32[]{:S(2)}, u32[]{:S(2)}) async-start(bf16[16,2,3072]{2,1,0:T(2,128)(2,1)} %reshape.859), calls=%async_computation | async-start | bytes 393216 | tf_op jit(solution)/shard_map/all_to_all | solution.py:123
  53.2 26.8 %copy-start.48 = (f32[4,128]{1,0:T(4,128)S(1)}, f32[4,128]{1,0:T(4,128)}, u32[]{:S(2)}) copy-start(f32[4,128]{1,0:T(4,128)} %param.11) | copy-start | bytes 6148
  53.2 19.7 %all-to-all-start.3 = ((bf16[16,2,7168]{2,1,0:T(2,128)(2,1)}), bf16[16,2,7168]{2,1,0:T(2,128)(2,1)S(1)}, u32[]{:S(2)}, u32[]{:S(2)}) async-start(bf16[16,2,7168]{2,1,0:T(2,128)(2,1)} %reshape.861), calls=%async_computation.3 | async-start | bytes 917504 | tf_op jit(solution)/shard_map/all_to_all | solution.py:126
  72.9 52.6 %all-to-all-start.1 = ((bf16[1,112,3,2048]{1,2,0,3:T(4,128)(2,1)}), bf16[1,112,3,2048]{1,2,0,3:T(4,128)(2,1)S(1)}, u32[]{:S(2)}, u32[]{:S(2)}) async-start(bf16[1,112,3,2048]{1,2,0,3:T(4,128)(2,1)} %copy.60), calls=%async_computation.1 | async-start | bytes 4194304 | tf_op jit(solution)/shard_map/all_to_all | solution.py:122
  78.6 75.6 %copy-start.39 = (pred[128]{0:T(512)(128)(4,1)}, pred[128]{0:T(512)(128)(4,1)S(1)}, u32[]{:S(2)}) copy-start(pred[128]{0:T(512)(128)(4,1)S(1)} %iota_compare_fusion.1) | copy-start | bytes 388
  78.7 75.6 %copy-start.41 = (f32[128]{0:T(128)}, f32[128]{0:T(128)S(1)}, u32[]{:S(2)}) copy-start(f32[128]{0:T(128)S(1)} %multiply_power_fusion) | copy-start | bytes 1540
  78.7 53.6 %copy-start.45 = (pred[128]{0:T(512)(128)(4,1)}, pred[128]{0:T(512)(128)(4,1)S(1)}, u32[]{:S(2)}) copy-start(pred[128]{0:T(512)(128)(4,1)S(1)} %get-tuple-element.163) | copy-start | bytes 388
  78.7 75.6 %copy-start.43 = (pred[128]{0:T(512)(128)(4,1)}, pred[128]{0:T(512)(128)(4,1)S(1)}, u32[]{:S(2)}) copy-start(pred[128]{0:T(512)(128)(4,1)S(1)} %get-tuple-element.162) | copy-start | bytes 388
  79.9 52.4 %copy-start.22 = (f32[2048]{0:T(1024)}, f32[2048]{0:T(1024)S(1)}, u32[]{:S(2)}) copy-start(f32[2048]{0:T(1024)S(1)} %get-tuple-element.160) | copy-start | bytes 24580
  79.9 52.4 %copy-start.24 = (f32[2048]{0:T(1024)}, f32[2048]{0:T(1024)S(1)}, u32[]{:S(2)}) copy-start(f32[2048]{0:T(1024)S(1)} %get-tuple-element.161) | copy-start | bytes 24580
  80.0 52.3 %copy-start.28 = (f32[128]{0:T(128)}, f32[128]{0:T(128)S(1)}, u32[]{:S(2)}) copy-start(f32[128]{0:T(128)S(1)} %get-tuple-element.153) | copy-start | bytes 1540
  80.0 52.3 %copy-start.35 = (f32[128]{0:T(128)}, f32[128]{0:T(128)S(1)}, u32[]{:S(2)}) copy-start(f32[128]{0:T(128)S(1)} %get-tuple-element.156) | copy-start | bytes 1540
  80.0 74.2 %copy-start.30 = (f32[128]{0:T(128)}, f32[128]{0:T(128)S(1)}, u32[]{:S(2)}) copy-start(f32[128]{0:T(128)S(1)} %get-tuple-element.154) | copy-start | bytes 1540
  80.0 74.2 %copy-start.32 = (f32[128]{0:T(128)}, f32[128]{0:T(128)S(1)}, u32[]{:S(2)}) copy-start(f32[128]{0:T(128)S(1)} %get-tuple-element.155) | copy-start | bytes 1540
  81.5 11.3 %copy-start.17 = (bf16[1,16,16,128]{3,2,1,0:T(8,128)(2,1)}, bf16[1,16,16,128]{3,2,1,0:T(8,128)(2,1)S(1)}, u32[]{:S(2)}) copy-start(bf16[1,16,16,128]{3,2,1,0:T(8,128)(2,1)S(1)} %copy.72) | copy-start | bytes 196612
  87.6 42.0 %copy-start.11 = (bf16[256,3,128]{0,2,1:T(8,128)(2,1)}, bf16[256,3,128]{0,2,1:T(8,128)(2,1)S(1)}, u32[]{:S(2)}) copy-start(bf16[256,3,128]{0,2,1:T(8,128)(2,1)S(1)} %copy.63) | copy-start | bytes 589828
  92.8 34.9 %copy-start.8 = (bf16[1,16,112,128]{3,2,1,0:T(8,128)(2,1)}, bf16[1,16,112,128]{3,2,1,0:T(8,128)(2,1)S(1)}, u32[]{:S(2)}) copy-start(bf16[1,16,112,128]{3,2,1,0:T(8,128)(2,1)S(1)} %copy.75) | copy-start | bytes 1376260
  129.8 11.2 %copy-start.19 = (f32[2048]{0:T(1024)}, f32[2048]{0:T(1024)S(1)}, u32[]{:S(2)}) copy-start(f32[2048]{0:T(1024)S(1)} %get-tuple-element.159) | copy-start | bytes 24580
  143.0 11.3 %copy-start.46 = (pred[128]{0:T(512)(128)(4,1)S(1)}, pred[128]{0:T(512)(128)(4,1)}, u32[]{:S(2)}) copy-start(pred[128]{0:T(512)(128)(4,1)} %copy-done.45) | copy-start | bytes 388
  162.1 41.9 %copy-start.12 = (f32[2048,1,127]{0,2,1:T(8,128)S(1)}, f32[2048,1,127]{0,2,1:T(8,128)}, u32[]{:S(2)}) copy-start(f32[2048,1,127]{0,2,1:T(8,128)} %get-tuple-element.143) | copy-start | bytes 3121156
  204.0 10.6 %copy-start.13 = (f32[2048,1,127]{0,2,1:T(8,128)S(1)}, f32[2048,1,127]{0,2,1:T(8,128)}, u32[]{:S(2)}) copy-start(f32[2048,1,127]{0,2,1:T(8,128)} %get-tuple-element.131) | copy-start | bytes 3121156
  241.3 13.2 %all-to-all-start.5 = ((bf16[1,256,4,128]{3,2,0,1:T(4,128)(2,1)}), bf16[1,256,4,128]{3,2,0,1:T(4,128)(2,1)S(1)}, u32[]{:S(2)}, u32[]{:S(2)}) async-start(bf16[1,256,4,128]{3,2,0,1:T(4,128)(2,1)} %copy.84), calls=%async_computation.5 | async-start | bytes 524288 | tf_op jit(solution)/shard_map/all_to_all | solution.py:150
  254.5 160.0 %all-to-all-start.4 = ((bf16[1,1792,4,128]{3,2,0,1:T(4,128)(2,1)}), bf16[1,1792,4,128]{3,2,0,1:T(4,128)(2,1)S(1)}, u32[]{:S(2)}, u32[]{:S(2)}) async-start(bf16[1,1792,4,128]{3,2,0,1:T(4,128)(2,1)} %copy.81), calls=%async_computation.4 | async-start | bytes 3670016 | tf_op jit(solution)/shard_map/all_to_all | solution.py:149
  (52 other events, 259.3 us)
